TPU v7x, 32 devices: a whole 2x2x4 slice. The times are simulated.
32 devices in a mesh: groups: 2 (over y), tensor: 8 (over z, x), seq: 2 (over core).
Axes of the slice: x: 2, y: 2, z: 4, core: 2. Of those that a mesh axis runs over, the one named last changes fastest.
Arguments:
- stored_hidden: bfloat16 [4, 64, 7168], P(('groups', 'seq'), None, 'tensor'), parts along dimension 0, may hold values from -6 to 6
- w_down_kv: bfloat16 [7168, 576], P('tensor'), may hold values from -0.0625 to 0.0625
- kv_gain: bfloat16 [512], replicated, may hold values from 0.5 to 1.5
- evicted_blocks: int32 [2], P('groups'), parts along dimension 0, may hold values from 0 to 127, as said below
- query_latent: bfloat16 [64, 1536], P(('groups', 'tensor')), parts along dimension 0, may hold values from -6 to 6
- w_up_q: bfloat16 [1536, 24576], P(None, 'tensor'), may hold values from -0.15625 to 0.15625
- w_key_absorb: bfloat16 [128, 128, 512], P('tensor'), may hold values from -0.5 to 0.5
- w_value: bfloat16 [128, 512, 128], P('tensor'), may hold values from -0.25 to 0.25
- query_positions: int32 [64], P('groups'), parts along dimension 0, may hold values from 16384 to 32767
- prefix_lengths: int32 [8], P('groups'), parts along dimension 0, may hold values from 4096 to 16384, as said below
- latent_cache: bfloat16 [32768, 576], P(('groups', 'seq')), parts along dimension 0, may hold values from -500 to 500
Outputs:
- rebuilt: bfloat16 [4, 64, 576], P(('groups', 'seq'), 'tensor'), parts along dimension 0
- attended: bfloat16 [64, 16384], P('groups', 'tensor'), parts along dimension 0
There are 2 independent parts, one for each index of `groups`. A program takes and returns all parts, laid end to end along the dimension named above; an argument that names none is the same for every part. Nothing has to cross between parts.
Inputs may be any that keep to these rules, and one draw needn't show every extreme that they name: `evicted_blocks`: distinct block numbers of the cached prefix. `prefix_lengths`: one request's length is exactly 16384.
All inputs are finite; a program needn't handle non-finite values.
Results may differ from a plain program's by a relative error of at most 0.012.
The roundings to bfloat16 on the way count: a program that leaves them out, or rounds other values in their place, can miss the bound.
Values may be sent and summed in bfloat16 or wider, within the bound.
A program may use at most 64 MiB of HBM per device.

v0:
```python
import functools
import numpy as np
import jax
import jax.numpy as jnp
from jax import lax
from jax.experimental import pallas as pl
from jax.experimental.pallas import tpu as pltpu
from jax.sharding import PartitionSpec as P

BLK = 128
NEG = -1e30
FLOOR = -1e20
FAR = 2**30
NORM_EPS = 1e-06
F32 = jnp.float32
BF16 = jnp.bfloat16
MESH = pl.DeviceIdType.MESH


def swap_halves(x):
    half = x.shape[-1] // 2
    return jnp.concatenate([x[:, half:], x[:, :half]], axis=-1)


def trig(pos, freq, rope_dim):
    angle = pos.astype(F32) * freq
    lane = lax.broadcasted_iota(jnp.int32, angle.shape, 1)
    sine = jnp.sin(angle)
    return jnp.cos(angle), jnp.where(lane < rope_dim // 2, -sine, sine)


def kernel(
    cfg,
    eb_hbm, qp_hbm, pf_hbm, freq_hbm, gain_hbm,
    hid_hbm, wd_hbm, ql_hbm, wq_hbm, wk_hbm, wv_hbm, kc_hbm,
    reb_ref, att_ref,
    eb_ref, qp_ref, pf_ref, freq_ref, gain_ref,
    hid, wd, ql, qlf, wq, wk, wv, kc,
    qf, part, rsum, rown, rall, fx, sb, mx_s, l_s, acc_s, osend, orecv,
    i_sem, w_sem, q_sem, c_sem, ql_ss, ql_rs, rs_ss, rs_rs, ag_ss, ag_rs, ex_ss, ex_rs,
):
    T, heads, nope, rank, rope_dim, Q, requests, nq, nb, bk, ng, kt = cfg
    me = lax.axis_index("tensor")
    sq = lax.axis_index("seq")
    other = 1 - sq
    head_qk = nope + rope_dim
    piece = ql_hbm.shape[0]
    half_rows = hid.shape[0]
    local = half_rows // T
    R = heads * Q
    n_evicted = eb_ref.shape[0]
    hq = heads // nq
    width = rank + rope_dim
    kd, nk = kc.shape
    extra = kd - width

    def far(d):
        return lax.rem(me + d, T)

    def near(d):
        return lax.rem(me + T - d, T)

    barrier = pltpu.get_barrier_semaphore()
    for d in range(1, T):
        pl.semaphore_signal(barrier, inc=1, device_id={"tensor": far(d)}, device_id_type=MESH)
    pl.semaphore_signal(barrier, inc=1, device_id={"seq": other}, device_id_type=MESH)

    small = [
        pltpu.make_async_copy(src, dst, i_sem.at[n])
        for n, (src, dst) in enumerate((
            (eb_hbm, eb_ref), (qp_hbm, qp_ref), (pf_hbm, pf_ref),
            (freq_hbm, freq_ref), (gain_hbm, gain_ref),
        ))
    ]
    own_q = pltpu.make_async_copy(ql_hbm, ql.at[me], w_sem.at[0])
    c_hid = pltpu.make_async_copy(hid_hbm.at[0], hid, w_sem.at[1])
    c_wd = pltpu.make_async_copy(wd_hbm, wd, w_sem.at[2])
    c_wk = pltpu.make_async_copy(wk_hbm, wk, w_sem.at[3])
    c_wv = pltpu.make_async_copy(wv_hbm, wv, w_sem.at[4])
    wide = hq * head_qk
    c_wq = [
        pltpu.make_async_copy(
            wq_hbm.at[:, pl.ds(i * wide, wide)], wq.at[:, pl.ds(i * wide, wide)], q_sem.at[i]
        )
        for i in range(nq)
    ]
    c_kc = [
        pltpu.make_async_copy(
            kc_hbm.at[:, pl.ds(i * bk, bk)], kc.at[pl.ds(0, width), pl.ds(i * bk, bk)],
            c_sem.at[i],
        )
        for i in range(nb)
    ]

    own_q.start()
    for c in small:
        c.start()
    c_hid.start()
    c_wd.start()
    for c in c_wq:
        c.start()
    c_wk.start()
    for c in c_kc:
        c.start()
    c_wv.start()

    def ql_copy(d, slot):
        return pltpu.make_async_remote_copy(
            src_ref=ql_hbm, dst_ref=ql.at[slot], send_sem=ql_ss.at[d], recv_sem=ql_rs.at[d],
            device_id={"tensor": far(d)}, device_id_type=MESH,
        )

    def rs_copy(d, slot):
        return pltpu.make_async_remote_copy(
            src_ref=part.at[far(d)], dst_ref=rsum.at[slot], send_sem=rs_ss.at[d],
            recv_sem=rs_rs.at[d], device_id={"tensor": far(d)}, device_id_type=MESH,
        )

    def ag_copy(d, slot):
        return pltpu.make_async_remote_copy(
            src_ref=rown, dst_ref=rall.at[slot], send_sem=ag_ss.at[d], recv_sem=ag_rs.at[d],
            device_id={"tensor": far(d)}, device_id_type=MESH,
        )

    pl.semaphore_wait(barrier, T)
    for d in range(1, T):
        ql_copy(d, me).start()

    for c in small:
        c.wait()
    freq = freq_ref[...]
    qrow = lax.broadcasted_iota(jnp.int32, (Q, 1), 0)
    qpos = lax.fori_loop(
        0, Q, lambda i, v: jnp.where(qrow == i, qp_ref[i], v), jnp.zeros((Q, 1), jnp.int32)
    )
    qcos, qsin = trig(qpos, freq, rope_dim)
    per = Q // requests
    belongs = lax.broadcasted_iota(jnp.int32, (Q, extra), 0) // per
    chosen = jnp.where(
        belongs == lax.broadcasted_iota(jnp.int32, (Q, extra), 1), 1.0, 0.0
    )
    flat0 = sq * half_rows + me * local
    rpos = (
        eb_ref[flat0 // BLK] * BLK + flat0 % BLK
        + lax.broadcasted_iota(jnp.int32, (local, 1), 0)
    )
    rcos, rsin = trig(rpos, freq, rope_dim)

    def limits(axis, shape):
        index = lax.broadcasted_iota(jnp.int32, shape, axis)
        limit = jnp.full(shape, FAR, jnp.int32)
        for r in range(requests):
            limit = jnp.where(index == r, pf_ref[r], limit)
        return jnp.where(index < requests, limit, 2 * (FAR - 1) + 1)

    pos = sq * nk + lax.broadcasted_iota(jnp.int32, (1, nk), 1)
    eff = pos
    for e in range(n_evicted):
        first = eb_ref[e] * BLK
        eff = jnp.where((pos >= first) & (pos < first + BLK), FAR, eff)
    kc[width:, :] = jnp.where(eff < limits(0, (extra, 1)), 0.0, NEG).astype(BF16)

    flat = sq * half_rows + lax.broadcasted_iota(jnp.int32, (half_rows, 1), 0)
    fpos = flat
    for e in range(n_evicted):
        inside = (flat >= e * BLK) & (flat < (e + 1) * BLK)
        fpos = jnp.where(inside, eb_ref[e] * BLK + flat - e * BLK, fpos)
    fbias = jnp.where(fpos < limits(1, (1, extra)), 0.0, NEG)

    c_hid.wait()
    c_wd.wait()
    partial = lax.dot_general(
        hid[...], wd[...], (((1,), (1,)), ((), ())), preferred_element_type=F32
    )
    for t in range(T):
        part[t] = partial[t * local:(t + 1) * local, :]
    rsum[me] = part[me]

    own_q.wait()
    for c in c_wq:
        c.wait()
    c_wk.wait()
    for d in range(1, T):
        ql_copy(d, near(d)).wait_recv()
    for d in range(1, T):
        rs_copy(d, me).start()
    for t in range(T):
        qlf[t * piece:(t + 1) * piece, :] = ql[t].astype(F32)
    queries = qlf[...].astype(BF16)
    scale = float(head_qk) ** (-0.5)

    def project(i):
        return jnp.dot(
            queries, wq[:, i * wide:(i + 1) * wide], preferred_element_type=F32
        )

    def absorb(i, proj):
        for j in range(hq):
            h = i * hq + j
            q_nope = proj[:, j * head_qk:j * head_qk + nope].astype(BF16)
            q_rope = proj[:, j * head_qk + nope:(j + 1) * head_qk]
            absorbed = jnp.dot(q_nope, wk[h], preferred_element_type=F32)
            qf[h * Q:(h + 1) * Q, :rank] = (absorbed * scale).astype(BF16)
            turned = q_rope * qcos + swap_halves(q_rope) * qsin
            qf[h * Q:(h + 1) * Q, rank:] = jnp.concatenate(
                [turned * scale, chosen], axis=-1
            ).astype(BF16)

    ahead = project(0)
    for i in range(1, nq):
        later = project(i)
        absorb(i - 1, ahead)
        ahead = later
    absorb(nq - 1, ahead)

    for c in c_kc:
        c.wait()
    nt = nk // kt
    LANES = 128
    early = max(1, (5 * nt) // 8)

    def fold(op, x):
        parts = [x[:, c * LANES:(c + 1) * LANES] for c in range(x.shape[1] // LANES)]
        while len(parts) > 1:
            parts = [
                op(parts[n], parts[n + 1]) if n + 1 < len(parts) else parts[n]
                for n in range(0, len(parts), 2)
            ]
        return parts[0]

    def score(t):
        cols = slice(t * kt, (t + 1) * kt)
        s = jnp.dot(qf[...], kc[:, cols], preferred_element_type=F32)
        sb[:, cols] = s
        top = fold(jnp.maximum, s)
        mx_s[...] = top if t == 0 else jnp.maximum(mx_s[...], top)

    for t in range(early):
        score(t)

    for d in range(1, T):
        rs_copy(d, near(d)).wait_recv()
    summed = rsum[0]
    for t in range(1, T):
        summed = summed + rsum[t]
    latent = summed[:, :rank]
    mean_square = jnp.mean(latent * latent, axis=-1, keepdims=True)
    normed = latent / jnp.sqrt(mean_square + NORM_EPS) * gain_ref[...].astype(F32).reshape(1, rank)
    tail = summed[:, rank:]
    turned = tail * rcos + swap_halves(tail) * rsin
    rown[:, :rank] = normed.astype(BF16)
    rown[:, rank:] = turned.astype(BF16)
    reb_ref[0] = rown[...]
    rall[me] = rown[...]
    for d in range(1, T):
        ag_copy(d, me).start()

    for t in range(early, nt):
        score(t)

    m_a = jnp.maximum(jnp.max(mx_s[...], axis=1, keepdims=True), FLOOR)
    mx_s[...] = jnp.broadcast_to(m_a, mx_s.shape)

    def weigh(t):
        top = mx_s[...]
        ps = [
            jnp.exp(sb[:, c:c + LANES] - top) for c in range(t * kt, (t + 1) * kt, LANES)
        ]
        p = jnp.concatenate(ps, axis=-1)
        total = fold(jnp.add, p)
        l_s[...] = total if t == 0 else l_s[...] + total
        out = lax.dot_general(
            p.astype(BF16), kc[:rank, t * kt:(t + 1) * kt], (((1,), (1,)), ((), ())),
            preferred_element_type=F32,
        )
        acc_s[...] = out if t == 0 else acc_s[...] + out

    for t in range(nt):
        weigh(t)

    for d in range(1, T):
        ag_copy(d, near(d)).wait_recv()
    fresh = jnp.concatenate([rall[t].astype(F32) for t in range(T)], axis=0)
    fx[:, :rank] = fresh[:, :rank].astype(BF16)
    fx[:, rank:] = jnp.concatenate([fresh[:, rank:], fbias], axis=-1).astype(BF16)
    s_f = lax.dot_general(
        qf[...], fx[...], (((1,), (1,)), ((), ())), preferred_element_type=F32
    )
    m_f = jnp.maximum(jnp.max(s_f, axis=1, keepdims=True), FLOOR)
    p_f = jnp.exp(s_f - m_f)
    l_f = jnp.sum(p_f, axis=1, keepdims=True)
    acc_f = jnp.dot(p_f.astype(BF16), fx[:, :rank], preferred_element_type=F32)
    l_a = jnp.sum(l_s[...], axis=1, keepdims=True)
    m_own = jnp.maximum(m_a, m_f)
    w_a, w_f = jnp.exp(m_a - m_own), jnp.exp(m_f - m_own)
    l_own = l_a * w_a + l_f * w_f

    vh = wv.shape[2]
    gcols = (heads // ng) * vh

    def ex_copy(g):
        cols = pl.ds(g * gcols, gcols) if g < ng else pl.ds(heads * vh, 128)
        return pltpu.make_async_remote_copy(
            src_ref=osend.at[:, cols], dst_ref=orecv.at[:, cols], send_sem=ex_ss.at[g],
            recv_sem=ex_rs.at[g], device_id={"seq": other}, device_id_type=MESH,
        )

    lane = lax.broadcasted_iota(jnp.int32, (Q, 128), 1)
    stats = jnp.zeros((Q, 128), F32)
    for h in range(heads):
        stats = jnp.where(lane == h, m_own[h * Q:(h + 1) * Q, :], stats)
        stats = jnp.where(lane == heads + h, l_own[h * Q:(h + 1) * Q, :], stats)
    osend[:, heads * vh:] = stats
    ex_copy(ng).start()
    c_wv.wait()
    for g in range(ng):
        for h in range(g * (heads // ng), (g + 1) * (heads // ng)):
            rows = slice(h * Q, (h + 1) * Q)
            a = acc_s[rows, :] * w_a[rows, :] + acc_f[rows, :] * w_f[rows, :]
            high = a.astype(BF16)
            low = (a - high.astype(F32)).astype(BF16)
            both = jnp.dot(
                jnp.concatenate([high, low], axis=0), wv[h], preferred_element_type=F32
            )
            osend[:, h * vh:(h + 1) * vh] = both[:Q] + both[Q:]
        ex_copy(g).start()

    ex_copy(ng).wait_recv()
    theirs = orecv[:, heads * vh:]
    m_a, m_b = stats[:, :heads], theirs[:, :heads]
    joint = jnp.maximum(m_a, m_b)
    e_a, e_b = jnp.exp(m_a - joint), jnp.exp(m_b - joint)
    total = e_a * stats[:, heads:2 * heads] + e_b * theirs[:, heads:2 * heads]
    e_a, e_b = e_a / total, e_b / total
    for g in range(ng):
        ex_copy(g).wait_recv()
        for h in range(g * (heads // ng), (g + 1) * (heads // ng)):
            cols = slice(h * vh, (h + 1) * vh)
            att_ref[:, cols] = (
                e_a[:, h:h + 1] * osend[:, cols] + e_b[:, h:h + 1] * orecv[:, cols]
            ).astype(BF16)

    for d in range(1, T):
        ql_copy(d, me).wait_send()
        rs_copy(d, me).wait_send()
        ag_copy(d, me).wait_send()
    for g in range(ng + 1):
        ex_copy(g).wait_send()


def hand_over(reb_in, att_in, reb_out, att_out):
    reb_out[...] = reb_in[...]
    att_out[...] = att_in[...]


def body(
    stored_hidden, w_down_kv, kv_gain, evicted_blocks, query_latent, w_up_q,
    w_key_absorb, w_value, query_positions, prefix_lengths, latent_cache,
):
    T = lax.axis_size("tensor")
    rank = kv_gain.shape[0]
    heads, nope = w_key_absorb.shape[:2]
    width = w_down_kv.shape[1]
    rope_dim = width - rank
    Q = query_positions.shape[0]
    requests = prefix_lengths.shape[0]
    half_rows = stored_hidden.shape[1]
    local = half_rows // T
    cache_rows = latent_cache.shape[0]
    bk = min(2048, cache_rows)
    nb = cache_rows // bk
    kt = min(1024, cache_rows)
    kd = rank + -(-(rope_dim + requests) // 128) * 128
    nq = max(1, heads // 4)
    ng = max(1, heads // 4)
    vh = w_value.shape[2]
    R = heads * Q
    half = np.arange(rope_dim // 2, dtype=np.float64) * (-2.0 / rope_dim)
    freq = jnp.asarray(np.tile(10000.0 ** half, 2)[None, :].astype(np.float32))
    cfg = (T, heads, nope, rank, rope_dim, Q, requests, nq, nb, bk, ng, kt)
    vmem = pl.BlockSpec(memory_space=pltpu.VMEM)
    hbm = pl.BlockSpec(memory_space=pl.ANY)
    dma = pltpu.SemaphoreType.DMA
    outs = pl.pallas_call(
        functools.partial(kernel, cfg),
        name="rebuild_attend",
        out_shape=(
            jax.ShapeDtypeStruct((1, local, width), BF16),
            jax.ShapeDtypeStruct((Q, heads * vh), BF16),
        ),
        in_specs=[hbm] * 12,
        out_specs=(vmem, vmem),
        scratch_shapes=[
            pltpu.SMEM(evicted_blocks.shape, jnp.int32),
            pltpu.SMEM(query_positions.shape, jnp.int32),
            pltpu.SMEM(prefix_lengths.shape, jnp.int32),
            pltpu.VMEM(freq.shape, F32),
            pltpu.VMEM(kv_gain.shape, BF16),
            pltpu.VMEM((half_rows, w_down_kv.shape[0]), BF16),
            pltpu.VMEM(w_down_kv.shape[::-1], BF16),
            pltpu.VMEM((T,) + query_latent.shape, BF16),
            pltpu.VMEM((Q, query_latent.shape[1]), F32),
            pltpu.VMEM(w_up_q.shape, BF16),
            pltpu.VMEM(w_key_absorb.shape, BF16),
            pltpu.VMEM(w_value.shape, BF16),
            pltpu.VMEM((kd, cache_rows), BF16),
            pltpu.VMEM((R, kd), BF16),
            pltpu.VMEM((T, local, width), F32),
            pltpu.VMEM((T, local, width), F32),
            pltpu.VMEM((local, width), BF16),
            pltpu.VMEM((T, local, width), BF16),
            pltpu.VMEM((half_rows, kd), BF16),
            pltpu.VMEM((R, cache_rows), F32),
            pltpu.VMEM((R, 128), F32),
            pltpu.VMEM((R, 128), F32),
            pltpu.VMEM((R, rank), F32),
            pltpu.VMEM((Q, heads * vh + 128), F32),
            pltpu.VMEM((Q, heads * vh + 128), F32),
            dma((5,)), dma((5,)), dma((nq,)), dma((nb,)),
            dma((T,)), dma((T,)), dma((T,)), dma((T,)), dma((T,)), dma((T,)),
            dma((ng + 1,)), dma((ng + 1,)),
        ],
        compiler_params=pltpu.CompilerParams(
            collective_id=0, has_side_effects=True, vmem_limit_bytes=60 * 1024 * 1024
        ),
    )(
        evicted_blocks, query_positions, prefix_lengths, freq, kv_gain,
        stored_hidden, w_down_kv.T, query_latent, w_up_q, w_key_absorb, w_value, latent_cache.T,
    )
    return pl.pallas_call(
        hand_over,
        name="hand_over",
        out_shape=tuple(jax.ShapeDtypeStruct(o.shape, o.dtype) for o in outs),
        in_specs=[vmem] * 2,
        out_specs=(vmem, vmem),
    )(*outs)


def solution(mesh):
    placed = (
        P(("groups", "seq"), None, "tensor"),
        P("tensor", None),
        P(),
        P("groups"),
        P(("groups", "tensor"), None),
        P(None, "tensor"),
        P("tensor", None, None),
        P("tensor", None, None),
        P("groups"),
        P("groups"),
        P(("groups", "seq"), None),
    )
    return jax.shard_map(
        body,
        mesh=mesh,
        in_specs=placed,
        out_specs=(P(("groups", "seq"), "tensor", None), P("groups", "tensor")),
        check_vma=False,
    )
```

profile of v0, /device:TPU:1, one launch (start us, length us, event | category | flops | bytes accessed | tf_op | source)
XLA Modules:
  0.0 30.7 jit_solution(7007158518577959838)
XLA Ops:
  1.3 27.8 %rebuild_attend.1 = (bf16[1,8,576]{2,1,0:T(8,128)(2,1)}, bf16[32,2048]{1,0:T(8,128)(2,1)}) custom-call(s32[1]{0:T(128)S(6)} %copy.14.eb_hbm, s32[32]{0:T(128)} %qp_hbm.1, s32[4]{0:T(128)} %pf_hbm.1, f32[1,64]{1,0:T(1,128)} %constant.2.clone.freq_hbm, bf16[512]{0:T(512)(128)(2,1)} %gain_hbm.1, bf16[1,64,896]{2,1,0:T(8,128)(2,1)} %hid_hbm.1, ...), custom_call_target="tpu_custom_call" | custom-call | tf_op jit(solution)/shard_map/rebuild_attend/pallas_call | solution.py:384
  29.1 1.6 %hand_over.1 = (bf16[1,8,576]{2,1,0:T(8,128)(2,1)}, bf16[32,2048]{1,0:T(8,128)(2,1)}) custom-call(bf16[1,8,576]{2,1,0:T(8,128)(2,1)} %get-tuple-element.4.reb_in, bf16[32,2048]{1,0:T(8,128)(2,1)} %get-tuple-element.5.att_in), custom_call_target="tpu_custom_call" | custom-call | tf_op jit(solution)/shard_map/hand_over/pallas_call | solution.py:430
where the time goes:
time: 30.9 us; the launch traced here: 30.7 us
  Pallas kernels  29.4 us (95%)
  between operations  1.29 us (4%)
    pallas_call x1, Pallas kernels, body(): pl.pallas_call(functools.partial(kernel, cfg), name='rebuild_attend', out...  27.8 us
    pallas_call x1, Pallas kernels, body(): pl.pallas_call(hand_over, name='hand_over', out_shape=tuple((jax.ShapeDty...  1.59 us

commit v1 on v0

v1 whole, which is shorter than its diff:
```python
import functools
import numpy as np
import jax
import jax.numpy as jnp
from jax import lax
from jax.experimental import pallas as pl
from jax.experimental.pallas import tpu as pltpu
from jax.sharding import PartitionSpec as P

BLK = 128
NEG = -1e30
FLOOR = -1e20
FAR = 2**30
NORM_EPS = 1e-06
F32 = jnp.float32
BF16 = jnp.bfloat16
MESH = pl.DeviceIdType.MESH


def swap_halves(x):
    half = x.shape[-1] // 2
    return jnp.concatenate([x[:, half:], x[:, :half]], axis=-1)


def trig(pos, freq, rope_dim):
    angle = pos.astype(F32) * freq
    lane = lax.broadcasted_iota(jnp.int32, angle.shape, 1)
    sine = jnp.sin(angle)
    return jnp.cos(angle), jnp.where(lane < rope_dim // 2, -sine, sine)


def kernel(
    cfg,
    eb_hbm, qp_hbm, pf_hbm, freq_hbm, gain_hbm,
    hid_hbm, wd_hbm, ql_hbm, wq_hbm, wk_hbm, wv_hbm, kc_hbm,
    reb_ref, att_ref,
    eb_ref, qp_ref, pf_ref, freq_ref, gain_ref,
    hid, wd, ql, qlf, wq, wk, wv, kc,
    qf, part, rsum, rown, rall, fx, sb, pb, mx_s, l_s, acc_s, osend, orecv,
    i_sem, w_sem, q_sem, c_sem, ql_ss, ql_rs, rs_ss, rs_rs, ag_ss, ag_rs,
    ex_ss, ex_rs, qx_ss, qx_rs,
):
    T, nope, rank, rope_dim, Q, requests, split, nq, nb, bk, ng, kt, ke = cfg
    me = lax.axis_index("tensor")
    sq = lax.axis_index("seq")
    other = 1 - sq
    head_qk = nope + rope_dim
    piece = ql_hbm.shape[0]
    half_rows = hid.shape[0]
    local = half_rows // T
    n_evicted = eb_ref.shape[0]
    hh, vh = wv.shape[1], wv.shape[3]
    hq = wk.shape[0] // nq
    width = rank + rope_dim
    kd, nk = kc.shape
    extra = kd - width
    halves = (sq, other) if split else (0, 1)
    facing = (1, 0) if split else (0, 1)

    def far(d):
        return lax.rem(me + d, T)

    def near(d):
        return lax.rem(me + T - d, T)

    barrier = pltpu.get_barrier_semaphore()
    for d in range(1, T):
        pl.semaphore_signal(barrier, inc=1, device_id={"tensor": far(d)}, device_id_type=MESH)
    pl.semaphore_signal(barrier, inc=1, device_id={"seq": other}, device_id_type=MESH)

    small = [
        pltpu.make_async_copy(src, dst, i_sem.at[n])
        for n, (src, dst) in enumerate((
            (eb_hbm, eb_ref), (qp_hbm, qp_ref), (pf_hbm, pf_ref),
            (freq_hbm, freq_ref), (gain_hbm, gain_ref),
        ))
    ]
    own_q = pltpu.make_async_copy(ql_hbm, ql.at[me], w_sem.at[0])
    c_hid = pltpu.make_async_copy(hid_hbm.at[0], hid, w_sem.at[1])
    c_wd = pltpu.make_async_copy(wd_hbm, wd, w_sem.at[2])
    wide = hq * head_qk
    first_head = sq * hh if split else 0
    c_wk = pltpu.make_async_copy(wk_hbm.at[pl.ds(first_head, nq * hq)], wk, w_sem.at[3])
    c_wv = [
        pltpu.make_async_copy(wv_hbm.at[pl.ds(halves[s] * hh, hh)], wv.at[s], w_sem.at[4 + s])
        for s in range(2)
    ]

    def c_wq_of(i):
        start = sq * (nq * wide) + i * wide if split else i * wide
        if split:
            start = pl.multiple_of(start, 128)
        return pltpu.make_async_copy(
            wq_hbm.at[:, pl.ds(start, wide)], wq.at[:, pl.ds(i * wide, wide)], q_sem.at[i]
        )

    c_wq = [c_wq_of(i) for i in range(nq)]
    c_kc = [
        pltpu.make_async_copy(
            kc_hbm.at[:, pl.ds(i * bk, bk)], kc.at[pl.ds(0, width), pl.ds(i * bk, bk)],
            c_sem.at[i],
        )
        for i in range(nb)
    ]

    own_q.start()
    for c in small:
        c.start()
    c_hid.start()
    c_wd.start()
    for c in c_wq:
        c.start()
    c_wk.start()
    for c in c_kc:
        c.start()
    for c in c_wv:
        c.start()

    def ql_copy(d, slot):
        return pltpu.make_async_remote_copy(
            src_ref=ql_hbm, dst_ref=ql.at[slot], send_sem=ql_ss.at[d], recv_sem=ql_rs.at[d],
            device_id={"tensor": far(d)}, device_id_type=MESH,
        )

    def rs_copy(d, slot):
        return pltpu.make_async_remote_copy(
            src_ref=part.at[far(d)], dst_ref=rsum.at[slot], send_sem=rs_ss.at[d],
            recv_sem=rs_rs.at[d], device_id={"tensor": far(d)}, device_id_type=MESH,
        )

    def qx_copy(i):
        size = hq * Q
        return pltpu.make_async_remote_copy(
            src_ref=qf.at[pl.ds(i * size, size)],
            dst_ref=qf.at[pl.ds((nq + i) * size, size)], send_sem=qx_ss.at[i],
            recv_sem=qx_rs.at[i], device_id={"seq": other}, device_id_type=MESH,
        )

    def ag_copy(d, slot):
        return pltpu.make_async_remote_copy(
            src_ref=rown, dst_ref=rall.at[slot], send_sem=ag_ss.at[d], recv_sem=ag_rs.at[d],
            device_id={"tensor": far(d)}, device_id_type=MESH,
        )

    pl.semaphore_wait(barrier, T)
    for d in range(1, T):
        ql_copy(d, me).start()

    for c in small:
        c.wait()
    freq = freq_ref[...]
    qrow = lax.broadcasted_iota(jnp.int32, (Q, 1), 0)
    qpos = lax.fori_loop(
        0, Q, lambda i, v: jnp.where(qrow == i, qp_ref[i], v), jnp.zeros((Q, 1), jnp.int32)
    )
    qcos, qsin = trig(qpos, freq, rope_dim)
    per = Q // requests
    belongs = lax.broadcasted_iota(jnp.int32, (Q, extra), 0) // per
    chosen = jnp.where(
        belongs == lax.broadcasted_iota(jnp.int32, (Q, extra), 1), 1.0, 0.0
    )
    flat0 = sq * half_rows + me * local
    rpos = (
        eb_ref[flat0 // BLK] * BLK + flat0 % BLK
        + lax.broadcasted_iota(jnp.int32, (local, 1), 0)
    )
    rcos, rsin = trig(rpos, freq, rope_dim)

    def limits(axis, shape):
        index = lax.broadcasted_iota(jnp.int32, shape, axis)
        limit = jnp.full(shape, FAR, jnp.int32)
        for r in range(requests):
            limit = jnp.where(index == r, pf_ref[r], limit)
        return jnp.where(index < requests, limit, 2 * (FAR - 1) + 1)

    pos = sq * nk + lax.broadcasted_iota(jnp.int32, (1, nk), 1)
    eff = pos
    for e in range(n_evicted):
        first = eb_ref[e] * BLK
        eff = jnp.where((pos >= first) & (pos < first + BLK), FAR, eff)
    kc[width:, :] = jnp.where(eff < limits(0, (extra, 1)), 0.0, NEG).astype(BF16)

    flat = sq * half_rows + lax.broadcasted_iota(jnp.int32, (half_rows, 1), 0)
    fpos = flat
    for e in range(n_evicted):
        inside = (flat >= e * BLK) & (flat < (e + 1) * BLK)
        fpos = jnp.where(inside, eb_ref[e] * BLK + flat - e * BLK, fpos)
    fbias = jnp.where(fpos < limits(1, (1, extra)), 0.0, NEG)

    c_hid.wait()
    c_wd.wait()
    partial = lax.dot_general(
        hid[...], wd[...], (((1,), (1,)), ((), ())), preferred_element_type=F32
    )
    for t in range(T):
        part[t] = partial[t * local:(t + 1) * local, :]
    rsum[me] = part[me]
    for d in range(1, T):
        rs_copy(d, me).start()

    own_q.wait()
    for c in c_wq:
        c.wait()
    c_wk.wait()
    for d in range(1, T):
        ql_copy(d, near(d)).wait_recv()
    for t in range(T):
        qlf[t * piece:(t + 1) * piece, :] = ql[t].astype(F32)
    queries = qlf[...].astype(BF16)
    scale = float(head_qk) ** (-0.5)

    def project(i):
        return jnp.dot(
            queries, wq[:, i * wide:(i + 1) * wide], preferred_element_type=F32
        )

    def absorb(i, proj):
        for j in range(hq):
            slot, h = divmod(i * hq + j, hh)
            at = slot * hh * Q + h * Q
            rows = slice(at, at + Q)
            q_nope = proj[:, j * head_qk:j * head_qk + nope].astype(BF16)
            q_rope = proj[:, j * head_qk + nope:(j + 1) * head_qk]
            absorbed = jnp.dot(q_nope, wk[i * hq + j], preferred_element_type=F32)
            qf[rows, :rank] = (absorbed * scale).astype(BF16)
            turned = q_rope * qcos + swap_halves(q_rope) * qsin
            qf[rows, rank:] = jnp.concatenate(
                [turned * scale, chosen], axis=-1
            ).astype(BF16)

    ahead = project(0)
    for i in range(1, nq):
        later = project(i)
        absorb(i - 1, ahead)
        ahead = later
        if split:
            qx_copy(i - 1).start()
    absorb(nq - 1, ahead)
    if split:
        qx_copy(nq - 1).start()

    for c in c_kc:
        c.wait()
    nt, ne = nk // kt, nk // ke
    kept = pb.shape[1] // ke
    LANES = 128

    def fold(op, x):
        parts = [x[:, c * LANES:(c + 1) * LANES] for c in range(x.shape[1] // LANES)]
        while len(parts) > 1:
            parts = [
                op(parts[n], parts[n + 1]) if n + 1 < len(parts) else parts[n]
                for n in range(0, len(parts), 2)
            ]
        return parts[0]

    R = hh * Q
    own, theirs, both = slice(0, R), slice(R, 2 * R), slice(0, 2 * R)

    def score(rows, t):
        cols = slice(t * kt, (t + 1) * kt)
        dots = jnp.dot(qf[rows, :], kc[:, cols], preferred_element_type=F32)
        sb[rows, cols] = dots
        top = fold(jnp.maximum, dots)
        mx_s[rows, :] = top if t == 0 else jnp.maximum(mx_s[rows, :], top)

    def highest(rows):
        top = jnp.maximum(jnp.max(mx_s[rows, :], axis=1, keepdims=True), FLOOR)
        mx_s[rows, :] = jnp.broadcast_to(top, mx_s[rows, :].shape)
        return top

    def weigh(rows, t):
        cols = slice(t * ke, (t + 1) * ke)
        top = mx_s[rows, :]
        ps = [jnp.exp(sb[rows, c:c + LANES] - top) for c in range(t * ke, (t + 1) * ke, LANES)]
        p = jnp.concatenate(ps, axis=-1)
        total = fold(jnp.add, p)
        l_s[rows, :] = total if t == 0 else l_s[rows, :] + total
        out = lax.dot_general(
            p.astype(BF16), kc[:rank, cols], (((1,), (1,)), ((), ())),
            preferred_element_type=F32,
        )
        acc_s[rows, :] = out if t == 0 else acc_s[rows, :] + out

    def ahead_of(rows, t):
        cols = slice(t * ke, (t + 1) * ke)
        top = mx_s[rows, :]
        ps = [jnp.exp(sb[rows, c:c + LANES] - top) for c in range(t * ke, (t + 1) * ke, LANES)]
        p = jnp.concatenate(ps, axis=-1)
        l_s[rows, :] = l_s[rows, :] + fold(jnp.add, p)
        n = t - (ne - kept)
        pb[rows, n * ke:(n + 1) * ke] = p.astype(BF16)

    def finish(rows):
        out = lax.dot_general(
            pb[rows, :], kc[:rank, (ne - kept) * ke:], (((1,), (1,)), ((), ())),
            preferred_element_type=F32,
        )
        acc_s[rows, :] = acc_s[rows, :] + out

    soon = max(1, (8 * nt) // 8)
    for t in range(soon):
        score(own, t)

    for d in range(1, T):
        rs_copy(d, near(d)).wait_recv()
    summed = rsum[0]
    for t in range(1, T):
        summed = summed + rsum[t]
    latent = summed[:, :rank]
    mean_square = jnp.mean(latent * latent, axis=-1, keepdims=True)
    normed = latent / jnp.sqrt(mean_square + NORM_EPS) * gain_ref[...].astype(F32).reshape(1, rank)
    tail = summed[:, rank:]
    turned = tail * rcos + swap_halves(tail) * rsin
    rown[:, :rank] = normed.astype(BF16)
    rown[:, rank:] = turned.astype(BF16)
    rall[me] = rown[...]
    for d in range(1, T):
        ag_copy(d, me).start()
    reb_ref[0] = rown[...]

    if split:
        for i in range(nq):
            qx_copy(i).wait_recv()
    for t in range(soon, nt):
        score(own, t)
    for t in range(nt):
        score(theirs, t)
    m_a = jnp.concatenate([highest(own), highest(theirs)], axis=0)
    for t in range(ne - kept):
        weigh(both, t)
    for t in range(ne - kept, ne):
        ahead_of(both, t)

    for d in range(1, T):
        ag_copy(d, near(d)).wait_recv()
    for c in c_wv:
        c.wait()
    fresh = jnp.concatenate([rall[t].astype(F32) for t in range(T)], axis=0)
    fx[:, :rank] = fresh[:, :rank].astype(BF16)
    fx[:, rank:] = jnp.concatenate([fresh[:, rank:], fbias], axis=-1).astype(BF16)

    s_f = lax.dot_general(
        qf[...], fx[...], (((1,), (1,)), ((), ())), preferred_element_type=F32
    )
    m_f = jnp.maximum(jnp.max(s_f, axis=1, keepdims=True), FLOOR)
    p_f = jnp.exp(s_f - m_f)
    l_f = jnp.sum(p_f, axis=1, keepdims=True)
    acc_f = jnp.dot(p_f.astype(BF16), fx[:, :rank], preferred_element_type=F32)
    m_own = jnp.maximum(m_a, m_f)
    w_a, w_f = jnp.exp(m_a - m_own), jnp.exp(m_f - m_own)

    def share(s):
        rows = slice(s * R, (s + 1) * R)
        l_own = jnp.sum(l_s[rows, :], axis=1, keepdims=True) * w_a[rows, :]
        l_own = l_own + l_f[rows, :] * w_f[rows, :]
        lane = lax.broadcasted_iota(jnp.int32, (Q, 128), 1)
        stats = jnp.zeros((Q, 128), F32)
        for h in range(hh):
            at = s * R + h * Q
            stats = jnp.where(lane == h, m_own[at:at + Q, :], stats)
            stats = jnp.where(lane == hh + h, l_own[h * Q:(h + 1) * Q, :], stats)
        osend[s, :, hh * vh:] = stats

    def expand(s, g):
        for h in range(g * (hh // ng), (g + 1) * (hh // ng)):
            rows = slice(s * R + h * Q, s * R + (h + 1) * Q)
            a = acc_s[rows, :] * w_a[rows, :] + acc_f[rows, :] * w_f[rows, :]
            high = a.astype(BF16)
            low = (a - high.astype(F32)).astype(BF16)
            both = jnp.dot(
                jnp.concatenate([high, low], axis=0), wv[s, h], preferred_element_type=F32
            )
            osend[s, :, h * vh:(h + 1) * vh] = both[:Q] + both[Q:]

    gcols = (hh // ng) * vh

    def cols_of(g):
        return pl.ds(g * gcols, gcols) if g < ng else pl.ds(hh * vh, 128)

    def ex_copy(s, g):
        n = s * (ng + 1) + g
        return pltpu.make_async_remote_copy(
            src_ref=osend.at[s, :, cols_of(g)], dst_ref=orecv.at[facing[s], :, cols_of(g)],
            send_sem=ex_ss.at[n], recv_sem=ex_rs.at[facing[s] * (ng + 1) + g],
            device_id={"seq": other}, device_id_type=MESH,
        )

    s_f = lax.dot_general(
        qf[...], fx[...], (((1,), (1,)), ((), ())), preferred_element_type=F32
    )
    m_f = jnp.maximum(jnp.max(s_f, axis=1, keepdims=True), FLOOR)
    p_f = jnp.exp(s_f - m_f)
    l_f = jnp.sum(p_f, axis=1, keepdims=True)
    acc_f = jnp.dot(p_f.astype(BF16), fx[:, :rank], preferred_element_type=F32)
    m_own = jnp.maximum(m_a, m_f)
    w_a, w_f = jnp.exp(m_a - m_own), jnp.exp(m_f - m_own)

    def share(s):
        rows = slice(s * R, (s + 1) * R)
        l_own = jnp.sum(l_s[rows, :], axis=1, keepdims=True) * w_a[rows, :]
        l_own = l_own + l_f[rows, :] * w_f[rows, :]
        lane = lax.broadcasted_iota(jnp.int32, (Q, 128), 1)
        stats = jnp.zeros((Q, 128), F32)
        for h in range(hh):
            at = s * R + h * Q
            stats = jnp.where(lane == h, m_own[at:at + Q, :], stats)
            stats = jnp.where(lane == hh + h, l_own[h * Q:(h + 1) * Q, :], stats)
        osend[s, :, hh * vh:] = stats

    def expand(s, g):
        for h in range(g * (hh // ng), (g + 1) * (hh // ng)):
            rows = slice(s * R + h * Q, s * R + (h + 1) * Q)
            a = acc_s[rows, :] * w_a[rows, :] + acc_f[rows, :] * w_f[rows, :]
            high = a.astype(BF16)
            low = (a - high.astype(F32)).astype(BF16)
            both = jnp.dot(
                jnp.concatenate([high, low], axis=0), wv[s, h], preferred_element_type=F32
            )
            osend[s, :, h * vh:(h + 1) * vh] = both[:Q] + both[Q:]

    gcols = (hh // ng) * vh

    def cols_of(g):
        return pl.ds(g * gcols, gcols) if g < ng else pl.ds(hh * vh, 128)

    def ex_copy(s, g):
        n = s * (ng + 1) + g
        return pltpu.make_async_remote_copy(
            src_ref=osend.at[s, :, cols_of(g)], dst_ref=orecv.at[facing[s], :, cols_of(g)],
            send_sem=ex_ss.at[n], recv_sem=ex_rs.at[facing[s] * (ng + 1) + g],
            device_id={"seq": other}, device_id_type=MESH,
        )

    def put(s, g):
        start = halves[s] * (hh * vh) + g * gcols
        if split:
            start = pl.multiple_of(start, 128)
        return pltpu.make_async_copy(
            att.at[s, :, cols_of(g)], att_hbm.at[:, pl.ds(start, gcols)], o_sem.at[s * ng + g]
        )

    finish(own)
    share(0)
    share(1)
    finish(theirs)
    for g in range(ng):
        expand(0, g)
    for s in range(2):
        ex_copy(s, ng).start()
    for g in range(ng):
        ex_copy(0, g).start()
    for g in range(ng):
        expand(1, g)
        ex_copy(1, g).start()

    for s in facing:
        ex_copy(facing[s], ng).wait_recv()
        stats, others = osend[s, :, hh * vh:], orecv[s, :, hh * vh:]
        m_o, m_t = stats[:, :hh], others[:, :hh]
        joint = jnp.maximum(m_o, m_t)
        e_o, e_t = jnp.exp(m_o - joint), jnp.exp(m_t - joint)
        total = e_o * stats[:, hh:2 * hh] + e_t * others[:, hh:2 * hh]
        e_o, e_t = e_o / total, e_t / total
        for g in range(ng):
            ex_copy(facing[s], g).wait_recv()
            for h in range(g * (hh // ng), (g + 1) * (hh // ng)):
                cols = slice(h * vh, (h + 1) * vh)
                start = halves[s] * (hh * vh) + h * vh
                if split:
                    start = pl.multiple_of(start, 128)
                att_ref[:, pl.ds(start, vh)] = (
                    e_o[:, h:h + 1] * osend[s, :, cols] + e_t[:, h:h + 1] * orecv[s, :, cols]
                ).astype(BF16)

    for d in range(1, T):
        ql_copy(d, me).wait_send()
        rs_copy(d, me).wait_send()
        ag_copy(d, me).wait_send()
    if split:
        for i in range(nq):
            qx_copy(i).wait_send()
    for s in range(2):
        for g in range(ng + 1):
            ex_copy(s, g).wait_send()


def hand_over(reb_in, att_in, reb_out, att_out, sems):
    copies = [
        pltpu.make_async_copy(att_in, att_out, sems.at[0]),
        pltpu.make_async_copy(reb_in, reb_out, sems.at[1]),
    ]
    for c in copies:
        c.start()
    for c in copies:
        c.wait()


def body(
    stored_hidden, w_down_kv, kv_gain, evicted_blocks, query_latent, w_up_q,
    w_key_absorb, w_value, query_positions, prefix_lengths, latent_cache,
):
    T = lax.axis_size("tensor")
    rank = kv_gain.shape[0]
    heads, nope = w_key_absorb.shape[:2]
    width = w_down_kv.shape[1]
    rope_dim = width - rank
    Q = query_positions.shape[0]
    requests = prefix_lengths.shape[0]
    half_rows = stored_hidden.shape[1]
    local = half_rows // T
    cache_rows = latent_cache.shape[0]
    bk = min(2048, cache_rows)
    nb = cache_rows // bk
    kt = min(1024, cache_rows)
    ke = min(1024, cache_rows)
    kd = rank + -(-(rope_dim + requests) // 128) * 128
    head_qk = nope + rope_dim
    hh = heads // 2
    split = (hh * head_qk) % 128 == 0
    held = hh if split else heads
    nq = max(1, held // 4)
    ng = max(1, hh // 4)
    vh = w_value.shape[2]
    R = hh * Q
    half = np.arange(rope_dim // 2, dtype=np.float64) * (-2.0 / rope_dim)
    freq = jnp.asarray(np.tile(10000.0 ** half, 2)[None, :].astype(np.float32))
    cfg = (T, nope, rank, rope_dim, Q, requests, split, nq, nb, bk, ng, kt, ke)
    hbm = pl.BlockSpec(memory_space=pl.ANY)
    dma = pltpu.SemaphoreType.DMA
    pieces = 2 * (ng + 1)
    rebuilt = jax.ShapeDtypeStruct((1, local, width), BF16)
    attended = jax.ShapeDtypeStruct((Q, heads * vh), BF16)
    outs = pl.pallas_call(
        functools.partial(kernel, cfg),
        name="rebuild_attend",
        out_shape=(rebuilt, attended),
        in_specs=[hbm] * 12,
        out_specs=(pl.BlockSpec(memory_space=pltpu.VMEM),) * 2,
        scratch_shapes=[
            pltpu.SMEM(evicted_blocks.shape, jnp.int32),
            pltpu.SMEM(query_positions.shape, jnp.int32),
            pltpu.SMEM(prefix_lengths.shape, jnp.int32),
            pltpu.VMEM(freq.shape, F32),
            pltpu.VMEM(kv_gain.shape, BF16),
            pltpu.VMEM((half_rows, w_down_kv.shape[0]), BF16),
            pltpu.VMEM(w_down_kv.shape[::-1], BF16),
            pltpu.VMEM((T,) + query_latent.shape, BF16),
            pltpu.VMEM((Q, query_latent.shape[1]), F32),
            pltpu.VMEM((w_up_q.shape[0], held * head_qk), BF16),
            pltpu.VMEM((held,) + w_key_absorb.shape[1:], BF16),
            pltpu.VMEM((2, hh) + w_value.shape[1:], BF16),
            pltpu.VMEM((kd, cache_rows), BF16),
            pltpu.VMEM((2 * R, kd), BF16),
            pltpu.VMEM((T, local, width), F32),
            pltpu.VMEM((T, local, width), F32),
            pltpu.VMEM((local, width), BF16),
            pltpu.VMEM((T, local, width), BF16),
            pltpu.VMEM((half_rows, kd), BF16),
            pltpu.VMEM((2 * R, cache_rows), F32),
            pltpu.VMEM((2 * R, 1 * ke), BF16),
            pltpu.VMEM((2 * R, 128), F32),
            pltpu.VMEM((2 * R, 128), F32),
            pltpu.VMEM((2 * R, rank), F32),
            pltpu.VMEM((2, Q, hh * vh + 128), F32),
            pltpu.VMEM((2, Q, hh * vh + 128), F32),
            dma((5,)), dma((6,)), dma((nq,)), dma((nb,)),
            dma((T,)), dma((T,)), dma((T,)), dma((T,)), dma((T,)), dma((T,)),
            dma((pieces,)), dma((pieces,)), dma((nq,)), dma((nq,)),
        ],
        compiler_params=pltpu.CompilerParams(
            collective_id=0, has_side_effects=True, vmem_limit_bytes=52000 * 1024
        ),
    )(
        evicted_blocks,
        *(pltpu.with_memory_space_constraint(x, pltpu.HBM) for x in (
            query_positions, prefix_lengths, freq, kv_gain, stored_hidden, w_down_kv.T,
            query_latent, w_up_q, w_key_absorb, w_value, latent_cache.T,
        )),
    )
    return pl.pallas_call(
        hand_over,
        name="hand_over",
        out_shape=(rebuilt, attended),
        in_specs=[hbm] * 2,
        out_specs=(hbm,) * 2,
        scratch_shapes=[dma((2,))],
        compiler_params=pltpu.CompilerParams(vmem_limit_bytes=52000 * 1024),
    )(*outs)


def solution(mesh):
    placed = (
        P(("groups", "seq"), None, "tensor"),
        P("tensor", None),
        P(),
        P("groups"),
        P(("groups", "tensor"), None),
        P(None, "tensor"),
        P("tensor", None, None),
        P("tensor", None, None),
        P("groups"),
        P("groups"),
        P(("groups", "seq"), None),
    )
    return jax.shard_map(
        body,
        mesh=mesh,
        in_specs=placed,
        out_specs=(P(("groups", "seq"), "tensor", None), P("groups", "tensor")),
        check_vma=False,
    )
```

time: 30.9 us -> 28.3 us (0.916)
  Pallas kernels: 29.4 us -> 26.9 us
    pallas_call x1, Pallas kernels: 27.8 us -> 26.2 us  [body(): pl.pallas_call(functools.partial(kernel, cfg), name='rebuild_attend', out...]
    pallas_call x1, Pallas kernels: 1.59 us -> 0.68 us  [body(): pl.pallas_call(hand_over, name='hand_over', out_shape=(rebuilt, attended)...]
where the time goes in v1:
time: 28.3 us; the launch traced here: 28.2 us
  Pallas kernels  26.9 us (95%)
  between operations  1.29 us (5%)
    pallas_call x1, Pallas kernels, body(): pl.pallas_call(functools.partial(kernel, cfg), name='rebuild_attend', out...  26.2 us
    pallas_call x1, Pallas kernels, body(): pl.pallas_call(hand_over, name='hand_over', out_shape=(rebuilt, attended)...  0.68 us

profile of v1, /device:TPU:1, one launch (start us, length us, event | category | flops | bytes accessed | tf_op | source)
XLA Modules:
  0.0 28.2 jit_solution(4509002118518961621)
XLA Ops:
  1.3 26.2 %rebuild_attend.1 = (bf16[1,8,576]{2,1,0:T(8,128)(2,1)S(1)}, bf16[32,2048]{1,0:T(8,128)(2,1)S(1)}) custom-call(s32[1]{0:T(128)S(6)} %copy.14.eb_hbm, s32[32]{0:T(128)} %qp_hbm.1, s32[4]{0:T(128)} %pf_hbm.1, f32[1,64]{1,0:T(1,128)} %constant.2.clone.freq_hbm, bf16[512]{0:T(512)(128)(2,1)} %gain_hbm.1, bf16[1,64,896]{2,1,0:T(8,128)(2,1)} %hid_hbm.1, ...), custom_call_target="tpu_custom_call" | custom-call | tf_op jit(solution)/shard_map/rebuild_attend/pallas_call | solution.py:534
  27.5 0.7 %hand_over.1 = (bf16[1,8,576]{2,1,0:T(8,128)(2,1)}, bf16[32,2048]{1,0:T(8,128)(2,1)}) custom-call(bf16[1,8,576]{2,1,0:T(8,128)(2,1)S(1)} %get-tuple-element.4.reb_in, bf16[32,2048]{1,0:T(8,128)(2,1)S(1)} %get-tuple-element.5.att_in), custom_call_target="tpu_custom_call" | custom-call | tf_op jit(solution)/shard_map/hand_over/pallas_call | solution.py:581

commit v2 on v1

--- a/solution.py
+++ b/solution.py
@@ -63,9 +63,18 @@
     def near(d):
         return lax.rem(me + T - d, T)
 
+    upper = lax.div(2 * me, T)
+
+    def distant(k):
+        low = k + lax.div(k + T - me, T)
+        high = T - 1 - k - lax.div(me + 1 + k, T)
+        return upper * low + (1 - upper) * high
+
     barrier = pltpu.get_barrier_semaphore()
-    for d in range(1, T):
-        pl.semaphore_signal(barrier, inc=1, device_id={"tensor": far(d)}, device_id_type=MESH)
+    for k in range(T - 1):
+        pl.semaphore_signal(
+            barrier, inc=1, device_id={"tensor": distant(k)}, device_id_type=MESH
+        )
     pl.semaphore_signal(barrier, inc=1, device_id={"seq": other}, device_id_type=MESH)
 
     small = [
@@ -116,10 +125,16 @@
     for c in c_wv:
         c.start()
 
-    def ql_copy(d, slot):
+    def ql_copy(k):
         return pltpu.make_async_remote_copy(
-            src_ref=ql_hbm, dst_ref=ql.at[slot], send_sem=ql_ss.at[d], recv_sem=ql_rs.at[d],
-            device_id={"tensor": far(d)}, device_id_type=MESH,
+            src_ref=ql_hbm, dst_ref=ql.at[me], send_sem=ql_ss.at[k], recv_sem=ql_rs.at[me],
+            device_id={"tensor": distant(k)}, device_id_type=MESH,
+        )
+
+    def ql_from(d):
+        return pltpu.make_async_remote_copy(
+            src_ref=ql_hbm, dst_ref=ql.at[near(d)], send_sem=ql_ss.at[0],
+            recv_sem=ql_rs.at[near(d)], device_id={"tensor": near(d)}, device_id_type=MESH,
         )
 
     def rs_copy(d, slot):
@@ -143,8 +158,8 @@
         )
 
     pl.semaphore_wait(barrier, T)
-    for d in range(1, T):
-        ql_copy(d, me).start()
+    for k in range(T - 1):
+        ql_copy(k).start()
 
     for c in small:
         c.wait()
@@ -203,7 +218,7 @@
         c.wait()
     c_wk.wait()
     for d in range(1, T):
-        ql_copy(d, near(d)).wait_recv()
+        ql_from(d).wait_recv()
     for t in range(T):
         qlf[t * piece:(t + 1) * piece, :] = ql[t].astype(F32)
     queries = qlf[...].astype(BF16)
@@ -242,7 +257,6 @@
     for c in c_kc:
         c.wait()
     nt, ne = nk // kt, nk // ke
-    kept = pb.shape[1] // ke
     LANES = 128
 
     def fold(op, x):
@@ -287,20 +301,25 @@
         top = mx_s[rows, :]
         ps = [jnp.exp(sb[rows, c:c + LANES] - top) for c in range(t * ke, (t + 1) * ke, LANES)]
         p = jnp.concatenate(ps, axis=-1)
-        l_s[rows, :] = l_s[rows, :] + fold(jnp.add, p)
-        n = t - (ne - kept)
-        pb[rows, n * ke:(n + 1) * ke] = p.astype(BF16)
-
-    def finish(rows):
+        total = fold(jnp.add, p)
+        l_s[rows, :] = total if t == 0 else l_s[rows, :] + total
+        pb[rows, :] = p.astype(BF16)
+
+    def finish(rows, t):
         out = lax.dot_general(
-            pb[rows, :], kc[:rank, (ne - kept) * ke:], (((1,), (1,)), ((), ())),
+            pb[rows, :], kc[:rank, t * ke:(t + 1) * ke], (((1,), (1,)), ((), ())),
             preferred_element_type=F32,
         )
-        acc_s[rows, :] = acc_s[rows, :] + out
-
-    soon = max(1, (8 * nt) // 8)
-    for t in range(soon):
+        acc_s[rows, :] = out if t == 0 else acc_s[rows, :] + out
+
+    lead, some = max(1, 6 * nt // 8), max(1, 3 * nt // 8)
+    for t in range(lead):
         score(own, t)
+    if split:
+        for i in range(nq):
+            qx_copy(i).wait_recv()
+    for t in range(some):
+        score(theirs, t)
 
     for d in range(1, T):
         rs_copy(d, near(d)).wait_recv()
@@ -319,23 +338,26 @@
         ag_copy(d, me).start()
     reb_ref[0] = rown[...]
 
-    if split:
-        for i in range(nq):
-            qx_copy(i).wait_recv()
-    for t in range(soon, nt):
+    for t in range(lead, nt):
         score(own, t)
-    for t in range(nt):
+    for t in range(some, nt):
         score(theirs, t)
     m_a = jnp.concatenate([highest(own), highest(theirs)], axis=0)
-    for t in range(ne - kept):
+    first = 1 if ne > 2 else 0
+    for t in range(first):
         weigh(both, t)
-    for t in range(ne - kept, ne):
-        ahead_of(both, t)
+    if ne > 1:
+        ahead_of(both, first)
+    c_wv[0].wait()
+    if ne > 1:
+        finish(both, first)
+    for t in range(first + 1, ne - 1):
+        weigh(both, t)
+    ahead_of(both, ne - 1)
 
     for d in range(1, T):
         ag_copy(d, near(d)).wait_recv()
-    for c in c_wv:
-        c.wait()
+    c_wv[1].wait()
     fresh = jnp.concatenate([rall[t].astype(F32) for t in range(T)], axis=0)
     fx[:, :rank] = fresh[:, :rank].astype(BF16)
     fx[:, rank:] = jnp.concatenate([fresh[:, rank:], fbias], axis=-1).astype(BF16)
@@ -440,10 +462,10 @@
             att.at[s, :, cols_of(g)], att_hbm.at[:, pl.ds(start, gcols)], o_sem.at[s * ng + g]
         )
 
-    finish(own)
+    finish(own, ne - 1)
     share(0)
     share(1)
-    finish(theirs)
+    finish(theirs, ne - 1)
     for g in range(ng):
         expand(0, g)
     for s in range(2):
@@ -454,27 +476,31 @@
         expand(1, g)
         ex_copy(1, g).start()
 
-    for s in facing:
-        ex_copy(facing[s], ng).wait_recv()
+    for s in range(2):
+        ex_copy(s, ng).wait_recv()
+    weights = []
+    for s in range(2):
         stats, others = osend[s, :, hh * vh:], orecv[s, :, hh * vh:]
         m_o, m_t = stats[:, :hh], others[:, :hh]
         joint = jnp.maximum(m_o, m_t)
         e_o, e_t = jnp.exp(m_o - joint), jnp.exp(m_t - joint)
         total = e_o * stats[:, hh:2 * hh] + e_t * others[:, hh:2 * hh]
-        e_o, e_t = e_o / total, e_t / total
+        weights.append((e_o / total, e_t / total))
+    for s in facing:
+        e_o, e_t = weights[s]
         for g in range(ng):
             ex_copy(facing[s], g).wait_recv()
-            for h in range(g * (hh // ng), (g + 1) * (hh // ng)):
-                cols = slice(h * vh, (h + 1) * vh)
-                start = halves[s] * (hh * vh) + h * vh
-                if split:
-                    start = pl.multiple_of(start, 128)
-                att_ref[:, pl.ds(start, vh)] = (
-                    e_o[:, h:h + 1] * osend[s, :, cols] + e_t[:, h:h + 1] * orecv[s, :, cols]
-                ).astype(BF16)
+        for h in range(hh):
+            cols = slice(h * vh, (h + 1) * vh)
+            start = halves[s] * (hh * vh) + h * vh
+            if split:
+                start = pl.multiple_of(start, 128)
+            att_ref[:, pl.ds(start, vh)] = (
+                e_o[:, h:h + 1] * osend[s, :, cols] + e_t[:, h:h + 1] * orecv[s, :, cols]
+            ).astype(BF16)
 
     for d in range(1, T):
-        ql_copy(d, me).wait_send()
+        ql_copy(d - 1).wait_send()
         rs_copy(d, me).wait_send()
         ag_copy(d, me).wait_send()
     if split:

time: 28.3 us -> 27.3 us (0.965)
  Pallas kernels: 26.9 us -> 25.9 us
    pallas_call x1, Pallas kernels: 26.2 us -> 25.2 us  [body(): pl.pallas_call(functools.partial(kernel, cfg), name='rebuild_attend', out...]
where the time goes in v2:
time: 27.3 us; the launch traced here: 27.2 us
  Pallas kernels  25.9 us (95%)
  between operations  1.29 us (5%)
    pallas_call x1, Pallas kernels, body(): pl.pallas_call(functools.partial(kernel, cfg), name='rebuild_attend', out...  25.2 us
    pallas_call x1, Pallas kernels, body(): pl.pallas_call(hand_over, name='hand_over', out_shape=(rebuilt, attended)...  0.68 us

profile of v2, /device:TPU:1, one launch (start us, length us, event | category | flops | bytes accessed | tf_op | source)
XLA Modules:
  0.0 27.2 jit_solution(4563460025988384117)
XLA Ops:
  1.3 25.2 %rebuild_attend.1 = (bf16[1,8,576]{2,1,0:T(8,128)(2,1)S(1)}, bf16[32,2048]{1,0:T(8,128)(2,1)S(1)}) custom-call(s32[1]{0:T(128)S(6)} %copy.14.eb_hbm, s32[32]{0:T(128)} %qp_hbm.1, s32[4]{0:T(128)} %pf_hbm.1, f32[1,64]{1,0:T(1,128)} %constant.2.clone.freq_hbm, bf16[512]{0:T(512)(128)(2,1)} %gain_hbm.1, bf16[1,64,896]{2,1,0:T(8,128)(2,1)} %hid_hbm.1, ...), custom_call_target="tpu_custom_call" | custom-call | tf_op jit(solution)/shard_map/rebuild_attend/pallas_call | solution.py:560
  26.5 0.7 %hand_over.1 = (bf16[1,8,576]{2,1,0:T(8,128)(2,1)}, bf16[32,2048]{1,0:T(8,128)(2,1)}) custom-call(bf16[1,8,576]{2,1,0:T(8,128)(2,1)S(1)} %get-tuple-element.4.reb_in, bf16[32,2048]{1,0:T(8,128)(2,1)S(1)} %get-tuple-element.5.att_in), custom_call_target="tpu_custom_call" | custom-call | tf_op jit(solution)/shard_map/hand_over/pallas_call | solution.py:607

commit v3 on v2

--- a/solution.py
+++ b/solution.py
@@ -60,8 +60,8 @@
     def far(d):
         return lax.rem(me + d, T)
 
-    def near(d):
-        return lax.rem(me + T - d, T)
+    def settle(ref, sem):
+        pltpu.make_async_copy(ref, ref, sem).wait()
 
     upper = lax.div(2 * me, T)
 
@@ -100,14 +100,14 @@
         if split:
             start = pl.multiple_of(start, 128)
         return pltpu.make_async_copy(
-            wq_hbm.at[:, pl.ds(start, wide)], wq.at[:, pl.ds(i * wide, wide)], q_sem.at[i]
+            wq_hbm.at[:, pl.ds(start, wide)], wq.at[:, pl.ds(i * wide, wide)], q_sem
         )
 
     c_wq = [c_wq_of(i) for i in range(nq)]
     c_kc = [
         pltpu.make_async_copy(
             kc_hbm.at[:, pl.ds(i * bk, bk)], kc.at[pl.ds(0, width), pl.ds(i * bk, bk)],
-            c_sem.at[i],
+            c_sem,
         )
         for i in range(nb)
     ]
@@ -127,20 +127,14 @@
 
     def ql_copy(k):
         return pltpu.make_async_remote_copy(
-            src_ref=ql_hbm, dst_ref=ql.at[me], send_sem=ql_ss.at[k], recv_sem=ql_rs.at[me],
+            src_ref=ql_hbm, dst_ref=ql.at[me], send_sem=ql_ss, recv_sem=ql_rs,
             device_id={"tensor": distant(k)}, device_id_type=MESH,
-        )
-
-    def ql_from(d):
-        return pltpu.make_async_remote_copy(
-            src_ref=ql_hbm, dst_ref=ql.at[near(d)], send_sem=ql_ss.at[0],
-            recv_sem=ql_rs.at[near(d)], device_id={"tensor": near(d)}, device_id_type=MESH,
         )
 
     def rs_copy(d, slot):
         return pltpu.make_async_remote_copy(
-            src_ref=part.at[far(d)], dst_ref=rsum.at[slot], send_sem=rs_ss.at[d],
-            recv_sem=rs_rs.at[d], device_id={"tensor": far(d)}, device_id_type=MESH,
+            src_ref=part.at[far(d)], dst_ref=rsum.at[slot], send_sem=rs_ss,
+            recv_sem=rs_rs, device_id={"tensor": far(d)}, device_id_type=MESH,
         )
 
     def qx_copy(i):
@@ -153,7 +147,7 @@
 
     def ag_copy(d, slot):
         return pltpu.make_async_remote_copy(
-            src_ref=rown, dst_ref=rall.at[slot], send_sem=ag_ss.at[d], recv_sem=ag_rs.at[d],
+            src_ref=rown, dst_ref=rall.at[slot], send_sem=ag_ss, recv_sem=ag_rs,
             device_id={"tensor": far(d)}, device_id_type=MESH,
         )
 
@@ -214,11 +208,9 @@
         rs_copy(d, me).start()
 
     own_q.wait()
-    for c in c_wq:
-        c.wait()
+    settle(wq, q_sem)
     c_wk.wait()
-    for d in range(1, T):
-        ql_from(d).wait_recv()
+    settle(ql.at[pl.ds(0, T - 1)], ql_rs)
     for t in range(T):
         qlf[t * piece:(t + 1) * piece, :] = ql[t].astype(F32)
     queries = qlf[...].astype(BF16)
@@ -254,8 +246,7 @@
     if split:
         qx_copy(nq - 1).start()
 
-    for c in c_kc:
-        c.wait()
+    settle(kc.at[pl.ds(0, width)], c_sem)
     nt, ne = nk // kt, nk // ke
     LANES = 128
 
@@ -321,8 +312,7 @@
     for t in range(some):
         score(theirs, t)
 
-    for d in range(1, T):
-        rs_copy(d, near(d)).wait_recv()
+    settle(rsum.at[pl.ds(0, T - 1)], rs_rs)
     summed = rsum[0]
     for t in range(1, T):
         summed = summed + rsum[t]
@@ -355,8 +345,7 @@
         weigh(both, t)
     ahead_of(both, ne - 1)
 
-    for d in range(1, T):
-        ag_copy(d, near(d)).wait_recv()
+    settle(rall.at[pl.ds(0, T - 1)], ag_rs)
     c_wv[1].wait()
     fresh = jnp.concatenate([rall[t].astype(F32) for t in range(T)], axis=0)
     fx[:, :rank] = fresh[:, :rank].astype(BF16)
@@ -401,10 +390,9 @@
         return pl.ds(g * gcols, gcols) if g < ng else pl.ds(hh * vh, 128)
 
     def ex_copy(s, g):
-        n = s * (ng + 1) + g
         return pltpu.make_async_remote_copy(
             src_ref=osend.at[s, :, cols_of(g)], dst_ref=orecv.at[facing[s], :, cols_of(g)],
-            send_sem=ex_ss.at[n], recv_sem=ex_rs.at[facing[s] * (ng + 1) + g],
+            send_sem=ex_ss, recv_sem=ex_rs.at[facing[s] * (ng + 1) + g],
             device_id={"seq": other}, device_id_type=MESH,
         )
 
@@ -447,10 +435,9 @@
         return pl.ds(g * gcols, gcols) if g < ng else pl.ds(hh * vh, 128)
 
     def ex_copy(s, g):
-        n = s * (ng + 1) + g
         return pltpu.make_async_remote_copy(
             src_ref=osend.at[s, :, cols_of(g)], dst_ref=orecv.at[facing[s], :, cols_of(g)],
-            send_sem=ex_ss.at[n], recv_sem=ex_rs.at[facing[s] * (ng + 1) + g],
+            send_sem=ex_ss, recv_sem=ex_rs.at[facing[s] * (ng + 1) + g],
             device_id={"seq": other}, device_id_type=MESH,
         )
 
@@ -499,16 +486,13 @@
                 e_o[:, h:h + 1] * osend[s, :, cols] + e_t[:, h:h + 1] * orecv[s, :, cols]
             ).astype(BF16)
 
-    for d in range(1, T):
-        ql_copy(d - 1).wait_send()
-        rs_copy(d, me).wait_send()
-        ag_copy(d, me).wait_send()
+    settle(ql.at[pl.ds(0, T - 1)], ql_ss)
+    settle(part.at[pl.ds(0, T - 1)], rs_ss)
+    settle(rall.at[pl.ds(0, T - 1)], ag_ss)
     if split:
         for i in range(nq):
             qx_copy(i).wait_send()
-    for s in range(2):
-        for g in range(ng + 1):
-            ex_copy(s, g).wait_send()
+    settle(osend, ex_ss)
 
 
 def hand_over(reb_in, att_in, reb_out, att_out, sems):
@@ -590,9 +574,8 @@
             pltpu.VMEM((2 * R, rank), F32),
             pltpu.VMEM((2, Q, hh * vh + 128), F32),
             pltpu.VMEM((2, Q, hh * vh + 128), F32),
-            dma((5,)), dma((6,)), dma((nq,)), dma((nb,)),
-            dma((T,)), dma((T,)), dma((T,)), dma((T,)), dma((T,)), dma((T,)),
-            dma((pieces,)), dma((pieces,)), dma((nq,)), dma((nq,)),
+            dma((5,)), dma((6,)), dma, dma, dma, dma, dma, dma, dma, dma,
+            dma, dma((pieces,)), dma((nq,)), dma((nq,)),
         ],
         compiler_params=pltpu.CompilerParams(
             collective_id=0, has_side_effects=True, vmem_limit_bytes=52000 * 1024

time: 27.3 us -> 26.8 us (0.982)
  Pallas kernels: 25.9 us -> 25.4 us
    pallas_call x1, Pallas kernels: 25.2 us -> 24.7 us  [body(): pl.pallas_call(functools.partial(kernel, cfg), name='rebuild_attend', out...]
where the time goes in v3:
time: 26.8 us; the launch traced here: 26.6 us
  Pallas kernels  25.4 us (95%)
  between operations  1.29 us (5%)
    pallas_call x1, Pallas kernels, body(): pl.pallas_call(functools.partial(kernel, cfg), name='rebuild_attend', out...  24.7 us
    pallas_call x1, Pallas kernels, body(): pl.pallas_call(hand_over, name='hand_over', out_shape=(rebuilt, attended)...  0.68 us

profile of v3, /device:TPU:1, one launch (start us, length us, event | category | flops | bytes accessed | tf_op | source)
XLA Modules:
  0.0 26.6 jit_solution(41171042645610595)
XLA Ops:
  1.3 24.7 %rebuild_attend.1 = (bf16[1,8,576]{2,1,0:T(8,128)(2,1)S(1)}, bf16[32,2048]{1,0:T(8,128)(2,1)S(1)}) custom-call(s32[1]{0:T(128)S(6)} %copy.14.eb_hbm, s32[32]{0:T(128)} %qp_hbm.1, s32[4]{0:T(128)} %pf_hbm.1, f32[1,64]{1,0:T(1,128)} %constant.2.clone.freq_hbm, bf16[512]{0:T(512)(128)(2,1)} %gain_hbm.1, bf16[1,64,896]{2,1,0:T(8,128)(2,1)} %hid_hbm.1, ...), custom_call_target="tpu_custom_call" | custom-call | tf_op jit(solution)/shard_map/rebuild_attend/pallas_call | solution.py:544
  26.0 0.7 %hand_over.1 = (bf16[1,8,576]{2,1,0:T(8,128)(2,1)}, bf16[32,2048]{1,0:T(8,128)(2,1)}) custom-call(bf16[1,8,576]{2,1,0:T(8,128)(2,1)S(1)} %get-tuple-element.4.reb_in, bf16[32,2048]{1,0:T(8,128)(2,1)S(1)} %get-tuple-element.5.att_in), custom_call_target="tpu_custom_call" | custom-call | tf_op jit(solution)/shard_map/hand_over/pallas_call | solution.py:590
